TPU v7x, 128 devices: a whole 4x4x4 slice. The times are simulated.
128 devices in a mesh: shell: 16 (over z, x), blk: 8 (over y, core).
Axes of the slice: x: 4, y: 4, z: 4, core: 2. Of those that a mesh axis runs over, the one named last changes fastest.
Arguments:
- cycle_fourier: bfloat16 [512, 2, 192, 1024], P('shell', None, None, 'blk'), may hold values from -6 to 6
- legendre: bfloat16 [192, 768, 1024], P('shell', None, 'blk'), may hold values from -0.1875 to 0.1875
- azimuth_orders: int32 [192], replicated, may hold values from 0 to 767, as said below
- multipole: int32 [768], P(('shell', 'blk')), may hold values from 0 to 767, each once
- bessel: bfloat16 [768, 512, 512], P(('shell', 'blk')), may hold values from -0.25 to 0.25
- signal_power: float32 [768, 512], P(('shell', 'blk')), may hold values from 0.1 to 10
- noise_power: float32 [768, 512], P(('shell', 'blk')), may hold values from 0.1 to 10
Outputs:
- filtered: bfloat16 [768, 512, 384], P('shell', 'blk')
Inputs may be any that keep to these rules, and one draw needn't show every extreme that they name: `azimuth_orders`: distinct orders; 0 and 767 always among them. Each multipole 0 to 767 appears once.
All inputs are finite; a program needn't handle non-finite values.
Results may differ from a plain program's by a relative error of at most 0.017.
Values may be sent and summed in bfloat16 or wider, within the bound.
A program may use at most 128 MiB of HBM per device.

v0:
```python
import jax
import jax.numpy as jnp
from jax import lax
from jax.sharding import PartitionSpec as P


def body(cycle_fourier, legendre, azimuth_orders, multipole, bessel, signal_power, noise_power):
    fields = lax.all_to_all(cycle_fourier, "shell", split_axis=2, concat_axis=0, tiled=True)
    shell_count = lax.axis_size("shell")
    group_count = lax.axis_size("blk")
    local_rows = legendre.shape[1] // (shell_count * group_count)
    partial_value = jnp.einsum(
        "jir,scjr->ijcs", legendre, fields, preferred_element_type=jnp.float32
    ).astype(jnp.bfloat16)
    moved = lax.all_to_all(partial_value, "shell", split_axis=0, concat_axis=1, tiled=True)
    summed = lax.psum_scatter(
        moved.astype(jnp.float32).astype(jnp.bfloat16), "blk", scatter_dimension=0, tiled=True
    )
    coeffs = summed
    allowed = multipole[:, None] >= azimuth_orders[None, :]
    coeffs = jnp.where(allowed[:, :, None, None], coeffs, jnp.zeros((), jnp.bfloat16))
    forward = jnp.einsum("iks,ijcs->ijck", bessel, coeffs, preferred_element_type=jnp.float32)
    wiener = signal_power / (signal_power + noise_power)
    scaled = (forward * wiener[:, None, None, :]).astype(jnp.bfloat16)
    synthesis = jnp.einsum("iks,ijck->isjc", bessel, scaled, preferred_element_type=jnp.float32)
    synthesis = synthesis.astype(jnp.bfloat16).reshape(
        local_rows, bessel.shape[2], 2 * azimuth_orders.shape[0]
    )
    return lax.all_to_all(synthesis, "blk", split_axis=1, concat_axis=0, tiled=True)


def solution(mesh):
    return jax.shard_map(
        body,
        mesh=mesh,
        in_specs=(
            P("shell", None, None, "blk"),
            P("shell", None, "blk"),
            P(),
            P(("shell", "blk")),
            P(("shell", "blk"), None, None),
            P(("shell", "blk"), None),
            P(("shell", "blk"), None),
        ),
        out_specs=P("shell", "blk", None),
        check_vma=False,
    )
```

profile of v0, /device:TPU:1, one launch (start us, length us, event | category | flops | bytes accessed | tf_op | source)
XLA Modules:
  0.0 553.9 jit_solution(11583145706594476009)
XLA Ops:
  6.5 0.0 copy-start
  6.5 0.0 reduce-scatter.2.cloned.1.call-start
  6.5 4.1 copy.23
  10.6 46.7 %all_to_all.54 = bf16[32,2,192,128]{3,0,1,2:T(8,128)(2,1)S(1)} all-to-all(bf16[32,2,192,128]{3,0,1,2:T(8,128)(2,1)S(1)} %copy.23), channel_id=1, replica_groups=mesh['shell'=16,'blk'=8] {'shell'}, dimensions={2} | all-to-all | bytes 6291456 | tf_op jit(solution)/shard_map/all_to_all | solution.py:8
  57.3 0.7 copy.25
  58.1 10.7 %convert_bitcast_fusion = bf16[768,12,2,512]{0,3,2,1:T(8,128)(2,1)} fusion(bf16[512,2,12,128]{3,0,1,2:T(8,128)(2,1)S(1)} %bitcast.39, bf16[12,768,128]{2,1,0:T(8,128)(2,1)} %param.8), kind=kOutput, calls=%fused_computation | convolution fusion | flops 2425356288 | bytes 24379392 | tf_op jit(solution)/shard_map/jir,scjr->ijcs/dot_general | solution.py:12
  68.8 46.5 %copy.26 = bf16[768,12,2,512]{3,2,1,0:T(2,128)(2,1)} copy(bf16[768,12,2,512]{0,3,2,1:T(8,128)(2,1)} %convert_bitcast_fusion) | data formatting | bytes 37748736 | tf_op jit(solution)/shard_map/convert_element_type | solution.py:14
  115.3 212.6 %all_to_all.55 = bf16[768,12,2,512]{3,2,1,0:T(2,128)(2,1)S(1)} all-to-all(bf16[768,12,2,512]{3,2,1,0:T(2,128)(2,1)} %copy.26), channel_id=1, replica_groups=mesh['shell'=16,'blk'=8] {'shell'}, dimensions={0} | all-to-all | bytes 37748736 | tf_op jit(solution)/shard_map/all_to_all | solution.py:15
  327.9 19.4 %copy.27 = bf16[768,12,2,512]{3,0,2,1:T(8,128)(2,1)S(1)} copy(bf16[768,12,2,512]{3,2,1,0:T(2,128)(2,1)S(1)} %all_to_all.55) | data formatting | bytes 37748736 | tf_op jit(solution)/shard_map/all_to_all | solution.py:15
  347.3 3.0 copy.28
  350.3 30.0 %copy.29 = bf16[48,192,2,512]{3,1,2,0:T(8,128)(2,1)} copy(bf16[48,192,2,512]{3,0,2,1:T(8,128)(2,1)S(1)} %bitcast.38) | data formatting | bytes 37748736 | tf_op jit(solution)/shard_map/all_to_all | solution.py:15
  380.3 0.0 reduce-scatter.2.cloned.1.call-update
  380.4 0.6 copy-done.3
  381.0 0.0 copy-done.4
  381.0 0.1 broadcast_compare_fusion
  381.1 0.0 copy-done.1
  381.1 0.0 copy-done.2
  381.1 99.6 %reduce-scatter.2.cloned.1.call-done = bf16[6,192,2,512]{3,1,2,0:T(8,128)(2,1)} async-done(((bf16[48,192,2,512]{3,1,2,0:T(8,128)(2,1)}), bf16[6,192,2,512]{3,1,2,0:T(8,128)(2,1)}) %reduce-scatter.2.cloned.1.call-update) | async-done | bytes 2359312 | tf_op jit(solution)/shard_map/reduce_scatter | solution.py:16
  480.7 5.7 %convert_bitcast_fusion.1 = bf16[6,512,192,2]{1,2,3,0:T(8,128)(2,1)} fusion(bf16[6,512,512]{2,1,0:T(8,128)(2,1)S(1)} %copy-done, f32[6,512]{1,0:T(8,128)S(1)} %add_divide_fusion, bf16[6,192,2,512]{3,1,2,0:T(8,128)(2,1)} %reduce-scatter.2.cloned.1.call-done, pred[6,192]{1,0:T(8,128)(4,1)S(1)} %broadcast_compare_fusion), kind=kOutput, calls=%fused_computation.7 | convolution fusion | flops 2420637696 | bytes 7877760 | tf_op jit(solution)/shard_map/iks,ijck->isjc/dot_general | solution.py:25
  486.5 5.5 copy.30
  492.0 6.1 %reshape.31 = bf16[6,512,384]{1,2,0:T(8,128)(2,1)} reshape(bf16[6,512,192,2]{1,3,2,0:T(2,128)(2,1)} %copy.30) | data formatting | bytes 4718592 | tf_op jit(solution)/shard_map/reshape | solution.py:26
  498.1 4.8 copy.31
  502.9 42.2 %all_to_all.56 = bf16[6,512,384]{2,0,1:T(8,128)(2,1)S(1)} all-to-all(bf16[6,512,384]{2,0,1:T(8,128)(2,1)} %copy.31), channel_id=1, replica_groups=mesh['shell'=16,'blk'=8] {'blk'}, dimensions={1} | all-to-all | bytes 4718592 | tf_op jit(solution)/shard_map/all_to_all | solution.py:29
  545.1 1.9 copy.33
  (6 shorter events, 0.0 us)
Async XLA Ops:
  6.5 474.2 %copy-start = (bf16[6,512,512]{2,1,0:T(8,128)(2,1)S(1)}, bf16[6,512,512]{2,1,0:T(8,128)(2,1)}, u32[]{:S(2)}) copy-start(bf16[6,512,512]{2,1,0:T(8,128)(2,1)} %param.11) | copy-start | bytes 9437188
  6.5 474.2 %reduce-scatter.2.cloned.1.call-start = ((), (), s32[]{:S(2)}) async-start(), calls=%async_computation.4 | async-start | bytes 21233664 | tf_op jit(solution)/shard_map/reduce_scatter | solution.py:16
  380.3 0.7 copy-start.3
  380.3 0.7 copy-start.4
  380.3 0.8 copy-start.1
  380.3 0.8 copy-start.2
Sparse Core Ops, SparseCore 0:
  380.5 100.2 reduce-scatter.1
where the time goes:
time: 556 us; the launch traced here: 554 us
  blocking collectives  302 us (54%)
  local copies, waits for them, and re-layouts  123 us (22%)
  waiting for transfers between devices  99.7 us (18%)
  matrix products  16.4 us (3%)
  between operations  13.4 us (2%)
    all_to_all x1, blocking collectives, body(): lax.all_to_all(partial_value, 'shell', split_axis=0, concat_axis=1, tiled...  213 us
    reduce_scatter x1, waiting for transfers between devices, body(): lax.psum_scatter(moved.astype(jnp.float32).astype(jnp.bfloat16), 'blk', s...  99.6 us
    all_to_all x3, local copies, waits for them, and re-layouts, body(): lax.all_to_all(partial_value, 'shell', split_axis=0, concat_axis=1, tiled...  52.4 us
    all_to_all x1, blocking collectives, body(): lax.all_to_all(cycle_fourier, 'shell', split_axis=2, concat_axis=0, tiled...  46.7 us
    convert_element_type x1, local copies, waits for them, and re-layouts, body(): partial_value = jnp.einsum('jir,scjr->ijcs', legendre, fields, preferred_...  46.5 us
    all_to_all x1, blocking collectives, body(): lax.all_to_all(synthesis, 'blk', split_axis=1, concat_axis=0, tiled=True)  42.2 us
  transfers between devices with their start and end apart: 1, of which 1 were waited for; matrix products, arithmetic and copies ran while one was open for 0% of the time, Pallas kernels for 0%

commit v1 on v0

v1 whole, which is shorter than its diff:
```python
import jax
import jax.numpy as jnp
from jax import lax
from jax.sharding import Mesh, PartitionSpec as P

PLANE = ("z", "x", "y")
ALL = ("z", "x", "y", "core")
SHELL = ("z", "x")
BLK = ("y", "core")


def body(cycle_fourier, legendre, azimuth_orders, multipole, bessel, signal_power, noise_power):
    shells, _, cols, cycles = cycle_fourier.shape
    ny = lax.axis_size("y")
    per = cols // (lax.axis_size("z") * lax.axis_size("x") * ny)
    planes = cols // per
    f = cycle_fourier.transpose(2, 1, 0, 3)
    f = lax.all_to_all(f, PLANE, split_axis=0, concat_axis=0, tiled=True)
    f = f.reshape(planes // ny, ny, per, 2, shells, cycles)
    rows = legendre.shape[1]
    t = lax.all_to_all(legendre, "y", split_axis=0, concat_axis=0, tiled=True)
    t = t.reshape(ny, per, rows, cycles)
    part = jnp.einsum("yjir,ayjcsr->cjias", t, f, preferred_element_type=jnp.float32)
    part = part.astype(jnp.bfloat16).reshape(2, per, rows, planes // ny * shells)
    both = lax.all_to_all(part, "core", split_axis=0, concat_axis=0, tiled=True)
    c = (both[0].astype(jnp.float32) + both[1].astype(jnp.float32)).astype(jnp.bfloat16)
    total = c.shape[-1]
    devices = planes * 2
    local = rows // devices
    c = c.reshape(per, devices, local, total).transpose(1, 2, 0, 3)
    c = lax.all_to_all(c, ALL, split_axis=0, concat_axis=0, tiled=True)
    c = c.reshape(planes, 2, local, per, total).transpose(2, 0, 3, 1, 4)
    coeffs = c.reshape(local, cols, 2, total)
    allowed = multipole[:, None] >= azimuth_orders[None, :]
    coeffs = jnp.where(allowed[:, :, None, None], coeffs, jnp.zeros((), jnp.bfloat16))
    coeffs = coeffs.reshape(local, cols * 2, total)
    forward = jnp.einsum("iks,ijs->ikj", bessel, coeffs, preferred_element_type=jnp.float32)
    wiener = signal_power / (signal_power + noise_power)
    scaled = (forward * wiener[:, :, None]).astype(jnp.bfloat16)
    out = jnp.einsum("iks,ikj->isj", bessel, scaled, preferred_element_type=jnp.float32)
    return lax.all_to_all(out.astype(jnp.bfloat16), BLK, split_axis=1, concat_axis=0, tiled=True)


def solution(mesh):
    fine = Mesh(mesh.devices.reshape(4, 4, 4, 2), ALL)
    return jax.shard_map(
        body,
        mesh=fine,
        in_specs=(
            P(SHELL, None, None, BLK),
            P(SHELL, None, BLK),
            P(),
            P(ALL),
            P(ALL, None, None),
            P(ALL, None),
            P(ALL, None),
        ),
        out_specs=P(SHELL, BLK, None),
        check_vma=False,
    )
```

time: 556 us -> 226 us (0.41)
  blocking collectives: 302 us -> 101 us
  local copies, waits for them, and re-layouts: 123 us -> 37.8 us
  waiting for transfers between devices: 99.7 us -> 64 us
  between operations: 13.4 us -> 0.09 us
  starting transfers between devices: 0.01 us -> 10.3 us
  matrix products: 16.4 us -> 9.76 us
    all_to_all x3, blocking collectives: 302 us -> 101 us  [the longest x1 48.1 us: body(): f = lax.all_to_all(f, PLANE, split_axis=0, concat_axis=0, tiled=True)]
    reduce_scatter x1 -> x0, waiting for transfers between devices: 99.6 us -> none  [body(): lax.psum_scatter(moved.astype(jnp.float32).astype(jnp.bfloat16), 'blk', s...]
    all_to_all x0 -> x2, waiting for transfers between devices: none -> 64 us  [the longest x1 40.7 us: body(): c = lax.all_to_all(c, ALL, split_axis=0, concat_axis=0, tiled=True)]
    all_to_all x5 -> x1, local copies, waits for them, and re-layouts: 55.1 us -> 1.92 us  [body(): lax.all_to_all(out.astype(jnp.bfloat16), BLK, split_axis=1, concat_axis=0...]
    convert_element_type x2 -> x4, local copies, waits for them, and re-layouts: 52 us -> 14.6 us  [the longest x2 9.36 us: body(): (both[0].astype(jnp.float32) + both[1].astype(jnp.float32)).astype(jnp.bf...]
    all_to_all x0 -> x2, starting transfers between devices: none -> 10.3 us  [the longest x1 5.26 us: body(): t = lax.all_to_all(legendre, 'y', split_axis=0, concat_axis=0, tiled=True)]
    transpose x0 -> x2, local copies, waits for them, and re-layouts: none -> 8.9 us  [the longest x1 5.11 us: body(): c = c.reshape(planes, 2, local, per, total).transpose(2, 0, 3, 1, 4)]
    dot_general x2, matrix products: 16.4 us -> 9.76 us  [the longest x1 5.18 us: body(): jnp.einsum('iks,ikj->isj', bessel, scaled, preferred_element_type=jnp.flo...]
  transfers between devices with their start and end apart: 1 -> 2, of which waited for: 1 -> 2; matrix products, arithmetic and copies ran while one was open for 0% -> 3% of each run, Pallas kernels for 0% -> 0%
where the time goes in v1:
time: 226 us; the launch traced here: 224 us
  blocking collectives  101 us (45%)
  waiting for transfers between devices  64 us (28%)
  local copies, waits for them, and re-layouts  37.8 us (17%)
  starting transfers between devices  10.3 us (5%)
  matrix products  9.76 us (4%)
    all_to_all x1, blocking collectives, body(): f = lax.all_to_all(f, PLANE, split_axis=0, concat_axis=0, tiled=True)  48.1 us
    all_to_all x1, blocking collectives, body(): lax.all_to_all(out.astype(jnp.bfloat16), BLK, split_axis=1, concat_axis=0...  42 us
    all_to_all x1, waiting for transfers between devices, body(): c = lax.all_to_all(c, ALL, split_axis=0, concat_axis=0, tiled=True)  40.7 us
    all_to_all x1, waiting for transfers between devices, body(): t = lax.all_to_all(legendre, 'y', split_axis=0, concat_axis=0, tiled=True)  23.3 us
    all_to_all x1, blocking collectives, body(): both = lax.all_to_all(part, 'core', split_axis=0, concat_axis=0, tiled=True)  10.5 us
    convert_element_type x2, local copies, waits for them, and re-layouts, body(): (both[0].astype(jnp.float32) + both[1].astype(jnp.float32)).astype(jnp.bf...  9.36 us
    reshape x1, local copies, waits for them, and re-layouts, body(): coeffs = c.reshape(local, cols, 2, total)  6.12 us
    unnamed x11, local copies, waits for them, and re-layouts  5.57 us
  transfers between devices with their start and end apart: 2, of which 2 were waited for; matrix products, arithmetic and copies ran while one was open for 3% of the time, Pallas kernels for 0%

profile of v1, /device:TPU:1, one launch (start us, length us, event | category | flops | bytes accessed | tf_op | source)
XLA Modules:
  0.0 224.5 jit_solution(8660560980968956102)
XLA Ops:
  0.0 0.0 copy-start
  0.0 5.3 %all-to-all-start.1 = ((bf16[12,768,128]{2,1,0:T(8,128)(2,1)}), bf16[12,768,128]{2,1,0:T(8,128)(2,1)}, u32[]{:S(2)}, u32[]{:S(2)}) async-start(bf16[12,768,128]{2,1,0:T(8,128)(2,1)} %param.8), calls=%async_computation.1 | async-start | bytes 4718592 | tf_op jit(solution)/shard_map/all_to_all | solution.py:21
  5.3 5.6 %copy.49 = bf16[32,2,192,128]{3,0,1,2:T(8,128)(2,1)} copy(bf16[32,2,192,128]{3,2,1,0:T(8,128)(2,1)} %param.7) | data formatting | bytes 6291456 | tf_op args[0]
  10.8 23.3 %all-to-all-done.1 = bf16[12,768,128]{2,1,0:T(8,128)(2,1)} async-done(((bf16[12,768,128]{2,1,0:T(8,128)(2,1)}), bf16[12,768,128]{2,1,0:T(8,128)(2,1)}, u32[]{:S(2)}, u32[]{:S(2)}) %all-to-all-start.1) | async-done | bytes 2359328 | tf_op jit(solution)/shard_map/all_to_all | solution.py:21
  34.1 48.1 %all_to_all.38 = bf16[192,2,32,128]{3,2,1,0:T(8,128)(2,1)S(1)} all-to-all(bf16[192,2,32,128]{3,2,1,0:T(8,128)(2,1)} %bitcast.32), channel_id=1, replica_groups=mesh['z'=4,'x'=4,'y'=4,'core'=2] {'z','x','y'}, dimensions={0} | all-to-all | bytes 6291456 | tf_op jit(solution)/shard_map/all_to_all | solution.py:18
  82.2 4.6 %fusion = bf16[2,3,768,16,32]{2,4,0,3,1:T(8,128)(2,1)S(1)} fusion(bf16[16,4,3,2,32,128]{5,4,3,2,1,0:T(8,128)(2,1)S(1)} %bitcast.36, bf16[4,3,768,128,1,1]{3,2,1,0,5,4:T(8,128)(2,1)} %bitcast.3), kind=kOutput, calls=%fused_computation.1 | convolution fusion | flops 2418278400 | bytes 10223616 | tf_op jit(solution)/shard_map/yjir,ayjcsr->cjias/dot_general | solution.py:23
  86.8 0.5 copy.28
  87.3 10.5 %all_to_all.39 = bf16[2,3,768,512]{2,3,1,0:T(8,128)(2,1)S(1)} all-to-all(bf16[2,3,768,512]{2,3,1,0:T(8,128)(2,1)S(1)} %bitcast.31), channel_id=1, replica_groups=mesh['z'=4,'x'=4,'y'=4,'core'=2] {'core'}, dimensions={0} | all-to-all | bytes 9437184 | tf_op jit(solution)/shard_map/all_to_all | solution.py:25
  97.7 1.9 add_convert_fusion
  99.7 4.3 %copy.29 = bf16[1,3,768,512]{3,2,1,0:T(8,128)(2,1)} copy(bf16[1,3,768,512]{2,3,1,0:T(8,128)(2,1)} %add_convert_fusion) | data formatting | bytes 4718592 | tf_op jit(solution)/shard_map/convert_element_type | solution.py:26
  104.0 5.0 %convert_element_type.38 = bf16[3,128,6,512]{3,2,1,0:T(8,128)(2,1)} reshape(bf16[1,3,768,512]{3,2,1,0:T(8,128)(2,1)} %copy.29) | data formatting | bytes 4718592 | tf_op jit(solution)/shard_map/convert_element_type | solution.py:26
  109.0 3.8 %copy.30 = bf16[128,6,3,512]{3,1,2,0:T(8,128)(2,1)} copy(bf16[128,6,3,512]{3,1,0,2:T(8,128)(2,1)} %bitcast.33) | data formatting | bytes 4718592 | tf_op jit(solution)/shard_map/transpose | solution.py:30
  112.8 5.0 %all-to-all-start.3 = ((bf16[128,6,3,512]{3,1,2,0:T(8,128)(2,1)}), bf16[128,6,3,512]{3,1,2,0:T(8,128)(2,1)}, u32[]{:S(2)}, u32[]{:S(2)}) async-start(bf16[128,6,3,512]{3,1,2,0:T(8,128)(2,1)} %copy.30), calls=%async_computation.3 | async-start | bytes 6291456 | tf_op jit(solution)/shard_map/all_to_all | solution.py:31
  117.9 0.1 broadcast_compare_fusion
  118.0 0.2 broadcast_in_dim.20
  118.2 0.4 broadcast_in_dim.21
  118.6 40.7 %all-to-all-done.3 = bf16[128,6,3,512]{3,1,2,0:T(8,128)(2,1)} async-done(((bf16[128,6,3,512]{3,1,2,0:T(8,128)(2,1)}), bf16[128,6,3,512]{3,1,2,0:T(8,128)(2,1)}, u32[]{:S(2)}, u32[]{:S(2)}) %all-to-all-start.3) | async-done | bytes 2359328 | tf_op jit(solution)/shard_map/all_to_all | solution.py:31
  159.3 5.1 %copy.50 = bf16[64,2,6,3,512]{4,1,3,0,2:T(2,128)(2,1)} copy(bf16[64,2,6,3,512]{4,2,3,1,0:T(8,128)(2,1)} %bitcast.9) | data formatting | bytes 4718592 | tf_op jit(solution)/shard_map/transpose | solution.py:32
  164.5 6.1 %reshape.57 = bf16[6,384,512]{2,1,0:T(8,128)(2,1)} reshape(bf16[6,64,3,2,512]{4,3,2,1,0:T(2,128)(2,1)} %bitcast.35) | data formatting | bytes 4718592 | tf_op jit(solution)/shard_map/reshape | solution.py:33
  170.6 0.0 copy-done
  170.6 5.2 %convert_bitcast_fusion = bf16[6,512,384]{1,2,0:T(8,128)(2,1)} fusion(bf16[6,512,512]{2,1,0:T(8,128)(2,1)S(1)} %copy-done, f32[6,512]{1,0:T(8,128)S(1)} %add_divide_fusion, bf16[6,384,512]{2,1,0:T(8,128)(2,1)} %reshape.57, pred[6,384]{1,0:T(8,128)(4,1)S(1)} %broadcast_in_dim.21), kind=kOutput, calls=%fused_computation.9 | convolution fusion | flops 2420637696 | bytes 7878912 | tf_op jit(solution)/shard_map/iks,ikj->isj/dot_general | solution.py:40
  175.8 4.8 %copy.33 = bf16[6,512,384]{2,0,1:T(8,128)(2,1)} copy(bf16[6,512,384]{1,2,0:T(8,128)(2,1)} %convert_bitcast_fusion) | data formatting | bytes 4718592 | tf_op jit(solution)/shard_map/convert_element_type | solution.py:41
  180.6 42.0 %all_to_all.40 = bf16[6,512,384]{2,0,1:T(8,128)(2,1)S(1)} all-to-all(bf16[6,512,384]{2,0,1:T(8,128)(2,1)} %copy.33), channel_id=1, replica_groups=mesh['z'=4,'x'=4,'y'=4,'core'=2] {'y','core'}, dimensions={1} | all-to-all | bytes 4718592 | tf_op jit(solution)/shard_map/all_to_all | solution.py:41
  222.6 1.9 copy.35
  (9 shorter events, 0.0 us)
Async XLA Ops:
  0.0 170.6 %copy-start = (bf16[6,512,512]{2,1,0:T(8,128)(2,1)S(1)}, bf16[6,512,512]{2,1,0:T(8,128)(2,1)}, u32[]{:S(2)}) copy-start(bf16[6,512,512]{2,1,0:T(8,128)(2,1)} %param.11) | copy-start | bytes 9437188
  0.0 34.1 %all-to-all-start.1 = ((bf16[12,768,128]{2,1,0:T(8,128)(2,1)}), bf16[12,768,128]{2,1,0:T(8,128)(2,1)}, u32[]{:S(2)}, u32[]{:S(2)}) async-start(bf16[12,768,128]{2,1,0:T(8,128)(2,1)} %param.8), calls=%async_computation.1 | async-start | bytes 4718592 | tf_op jit(solution)/shard_map/all_to_all | solution.py:21
  112.8 5.0 %copy-start.3 = (s32[192]{0:T(256)S(1)}, s32[192]{0:T(256)}, u32[]{:S(2)}) copy-start(s32[192]{0:T(256)} %param.9) | copy-start | bytes 2308
  112.8 5.0 %copy-start.4 = (s32[6]{0:T(128)S(1)}, s32[6]{0:T(128)}, u32[]{:S(2)}) copy-start(s32[6]{0:T(128)} %param.10) | copy-start | bytes 76
  112.8 5.8 %copy-start.1 = (f32[6,512]{1,0:T(8,128)S(1)}, f32[6,512]{1,0:T(8,128)}, u32[]{:S(2)}) copy-start(f32[6,512]{1,0:T(8,128)} %param.12) | copy-start | bytes 36868
  112.8 5.8 %copy-start.2 = (f32[6,512]{1,0:T(8,128)S(1)}, f32[6,512]{1,0:T(8,128)}, u32[]{:S(2)}) copy-start(f32[6,512]{1,0:T(8,128)} %param.13) | copy-start | bytes 36868
  112.8 46.5 %all-to-all-start.3 = ((bf16[128,6,3,512]{3,1,2,0:T(8,128)(2,1)}), bf16[128,6,3,512]{3,1,2,0:T(8,128)(2,1)}, u32[]{:S(2)}, u32[]{:S(2)}) async-start(bf16[128,6,3,512]{3,1,2,0:T(8,128)(2,1)} %copy.30), calls=%async_computation.3 | async-start | bytes 6291456 | tf_op jit(solution)/shard_map/all_to_all | solution.py:31

commit v2 on v1

v2 whole, which is shorter than its diff:
```python
import jax
import jax.numpy as jnp
from jax import lax
from jax.experimental import pallas as pl
from jax.experimental.pallas import tpu as pltpu
from jax.sharding import Mesh, PartitionSpec as P

ALL = ("z", "x", "y", "core")
SHELL = ("z", "x")
BLK = ("y", "core")
MESH = pl.DeviceIdType.MESH
BF16, F32 = jnp.bfloat16, jnp.float32
ROWS, CYC, SH = 768, 128, 32
NP, ND, PER = 64, 128, 3


def place():
    return tuple(lax.axis_index(n) for n in ALL)


def remote(src, dst, send, recv, z, x, y, c):
    return pltpu.make_async_remote_copy(
        src_ref=src, dst_ref=dst, send_sem=send, recv_sem=recv,
        device_id=(z, x, y, c), device_id_type=MESH,
    )


def drain(ref, sem):
    pltpu.make_async_copy(ref, ref, sem).wait()


def gather_kernel(f_ref, l_ref, out_ref, fr, lr, ps, pr, cf, cs,
                  f_send, f_recv, l_send, l_recv, p_send, p_recv, c_send, c_recv):
    z, x, y, c = place()
    plane = (z * 4 + x) * 4 + y
    me = plane * 2 + c
    barrier = pltpu.get_barrier_semaphore()

    def greet(d, _):
        pl.semaphore_signal(
            barrier, inc=1, device_id_type=MESH,
            device_id=((z + d // 32) % 4, (x + d // 8) % 4, (y + d // 2) % 4, (c + d) % 2),
        )
        return 0

    lax.fori_loop(1, ND, greet, 0)
    pl.semaphore_wait(barrier, ND - 1)

    for j in range(PER):
        for d in (2, 1, 3):
            ty = (y + d) % 4
            remote(l_ref.at[ty * PER + j], lr.at[j, y], l_send.at[j], l_recv.at[j], z, x, ty, c).start()
        pltpu.make_async_copy(l_ref.at[y * PER + j], lr.at[j, y], l_recv.at[j]).start()

        def send(d, _, j=j):
            tz, tx, ty = (z + d // 16) % 4, (x + d // 4) % 4, (y + d) % 4
            t = (tz * 4 + tx) * 4 + ty
            remote(f_ref.at[t * PER + j], fr.at[j, z * 4 + x, y], f_send.at[j], f_recv.at[j], tz, tx, ty, c).start()
            return 0

        lax.fori_loop(1, NP, send, 0)
        pltpu.make_async_copy(f_ref.at[plane * PER + j], fr.at[j, z * 4 + x, y], f_recv.at[j]).start()

    def half(j, part, m):
        lhs = jnp.concatenate([lr[j, b, pl.ds(m * 128, 128), :] for b in range(4)], axis=1)
        rhs = jnp.concatenate(
            [fr[j, :, b, part].reshape(16 * SH, CYC) for b in range(4)], axis=1
        )
        return lax.dot_general(lhs, rhs, (((1,), (1,)), ((), ())), preferred_element_type=F32)

    def spread(j, part):
        def step(m, _):
            acc = half(j, part, m)
            for q in range(4):
                cf[pl.ds(m * 512 + q, 128, stride=4), :] = acc[:, q * 128:(q + 1) * 128]
            return 0

        lax.fori_loop(0, ROWS // 128, step, 0)

    for j in range(PER):
        drain(lr.at[j], l_recv.at[j])
        drain(fr.at[j], f_recv.at[j])
        spread(j, 1 - c)

        def keep(m, _, j=j):
            rows = pl.ds(m * 512, 512)
            ps[j, rows, :] = cf[rows, :].astype(BF16)
            return 0

        lax.fori_loop(0, ROWS // 128, keep, 0)
        swap = remote(ps.at[j], pr.at[j], p_send.at[j], p_recv.at[j], z, x, y, 1 - c)
        swap.start()
        spread(j, c)
        swap.wait_recv()

        def add(m, _, j=j):
            rows = pl.ds(m * 512, 512)
            cs[j, rows, :] = (cf[rows, :] + pr[j, rows, :].astype(F32)).astype(BF16)
            return 0

        lax.fori_loop(0, ROWS // 128, add, 0)

        def post(d, _, j=j):
            tz, tx, ty, tc = (z + d // 32) % 4, (x + d // 8) % 4, (y + d // 2) % 4, (c + d) % 2
            t = ((tz * 4 + tx) * 4 + ty) * 2 + tc
            remote(cs.at[j, pl.ds(t * 24, 24)], out_ref.at[j, me], c_send.at[j], c_recv.at[j], tz, tx, ty, tc).start()
            return 0

        lax.fori_loop(1, ND, post, 0)
        pltpu.make_async_copy(cs.at[j, pl.ds(me * 24, 24)], out_ref.at[j, me], c_recv.at[j]).start()

    for j in range(PER):
        drain(out_ref.at[j], c_recv.at[j])
        drain(lr.at[j, pl.ds(0, 3)], l_send.at[j])
        drain(f_ref.at[pl.ds(0, NP - 1)], f_send.at[j])
        drain(out_ref.at[j, pl.ds(0, ND - 1)], c_send.at[j])
        remote(ps.at[j], pr.at[j], p_send.at[j], p_recv.at[j], z, x, y, 1 - c).wait_send()


def gather(f, t):
    dma = pltpu.SemaphoreType.DMA
    return pl.pallas_call(
        gather_kernel,
        out_shape=jax.ShapeDtypeStruct((PER, ND, 24, 128), BF16),
        in_specs=[pl.BlockSpec(memory_space=pl.ANY)] * 2,
        out_specs=pl.BlockSpec(memory_space=pl.ANY),
        scratch_shapes=[
            pltpu.VMEM((PER, 16, 4, 2, SH, CYC), BF16),
            pltpu.VMEM((PER, 4, ROWS, CYC), BF16),
            pltpu.VMEM((PER, ROWS * 4, 128), BF16),
            pltpu.VMEM((PER, ROWS * 4, 128), BF16),
            pltpu.VMEM((ROWS * 4, 128), F32),
            pltpu.VMEM((PER, ROWS * 4, 128), BF16),
        ] + [dma((PER,))] * 8,
        compiler_params=pltpu.CompilerParams(collective_id=0, has_side_effects=True, vmem_limit_bytes=40 * 2**20),
        name="gather",
    )(f, t)


def radial_kernel(c_ref, b_ref, s_ref, n_ref, k_ref, out_ref, xf, xi, os, o_send, o_recv):
    z, x, y, c = place()
    blk = y * 2 + c
    barrier = pltpu.get_barrier_semaphore()
    for d in range(1, 8):
        pl.semaphore_signal(
            barrier, inc=1, device_id_type=MESH, device_id=(z, x, (y + d // 2) % 4, (c + d) % 2)
        )

    def widen(m, _):
        for j in range(PER):
            xf[pl.ds((j * 8 + m) * 384, 384), :] = c_ref[j, pl.ds(m * 16, 16)].reshape(384, 128).astype(F32)
        return 0

    lax.fori_loop(0, 8, widen, 0)
    pl.semaphore_wait(barrier, 7)

    def row(i, _):
        for q in range(4):
            for j in range(PER):
                for h in range(2):
                    xi[q, pl.ds(2 * j + h, 64, stride=6), :] = xf[pl.ds(j * 3072 + h * 24 + i * 4 + q, 64, stride=48), :]
        rows = jnp.concatenate([xi[q].astype(BF16) for q in range(4)], axis=1)
        basis = b_ref[i]
        forward = lax.dot_general(rows, basis, (((1,), (1,)), ((), ())), preferred_element_type=F32)
        power = s_ref[pl.ds(i, 1), :]
        scaled = (forward * (power / (power + n_ref[pl.ds(i, 1), :]))).astype(BF16)
        out = lax.dot_general(basis, scaled, (((0,), (1,)), ((), ())), preferred_element_type=F32)
        out = jnp.where(k_ref[pl.ds(i, 1), :] > 0.5, out, 0.0)
        os[i] = out.astype(BF16)
        for d in range(1, 8):
            ty, tc = (y + d // 2) % 4, (c + d) % 2
            remote(os.at[i, pl.ds((ty * 2 + tc) * 64, 64)], out_ref.at[blk * 6 + i], o_send, o_recv, z, x, ty, tc).start()
        pltpu.make_async_copy(os.at[i, pl.ds(blk * 64, 64)], out_ref.at[blk * 6 + i], o_recv).start()
        return 0

    lax.fori_loop(0, 6, row, 0)
    drain(out_ref, o_recv)
    drain(out_ref.at[pl.ds(0, 42)], o_send)


def radial(coeffs, bessel, signal, noise, keep):
    dma = pltpu.SemaphoreType.DMA
    return pl.pallas_call(
        radial_kernel,
        out_shape=jax.ShapeDtypeStruct((48, 64, 384), BF16),
        in_specs=[pl.BlockSpec(memory_space=pltpu.VMEM)] * 5,
        out_specs=pl.BlockSpec(memory_space=pl.ANY),
        scratch_shapes=[
            pltpu.VMEM((PER * ND * 24, 128), F32),
            pltpu.VMEM((4, 384, 128), F32),
            pltpu.VMEM((6, 512, 384), BF16),
            dma, dma,
        ],
        compiler_params=pltpu.CompilerParams(collective_id=1, has_side_effects=True, vmem_limit_bytes=40 * 2**20),
        name="radial",
    )(coeffs, bessel, signal, noise, keep)


def body(cycle_fourier, legendre, azimuth_orders, multipole, bessel, signal_power, noise_power):
    coeffs = gather(cycle_fourier.transpose(2, 1, 0, 3), legendre)
    allowed = multipole[:, None] >= jnp.repeat(azimuth_orders, 2)[None, :]
    return radial(coeffs, bessel, signal_power, noise_power, allowed.astype(F32))


def solution(mesh):
    fine = Mesh(mesh.devices.reshape(4, 4, 4, 2), ALL)
    return jax.shard_map(
        body,
        mesh=fine,
        in_specs=(
            P(SHELL, None, None, BLK),
            P(SHELL, None, BLK),
            P(),
            P(ALL),
            P(ALL, None, None),
            P(ALL, None),
            P(ALL, None),
        ),
        out_specs=P(SHELL, BLK, None),
        check_vma=False,
    )
```

time: 226 us -> 146 us (0.65)
  Pallas kernels: 0 us -> 138 us
  blocking collectives: 101 us -> 0 us
  waiting for transfers between devices: 64 us -> 0 us
  local copies, waits for them, and re-layouts: 37.8 us -> 7.61 us
  starting transfers between devices: 10.3 us -> 0 us
  matrix products: 9.76 us -> 0 us
    pallas_call x0 -> x2, Pallas kernels: none -> 138 us  [the longest x1 108 us: gather(): pl.pallas_call(gather_kernel, out_shape=jax.ShapeDtypeStruct((PER, ND, 24...]
    all_to_all x3 -> x0, blocking collectives: 101 us -> none  [the longest x1 48.1 us: body(): f = lax.all_to_all(f, PLANE, split_axis=0, concat_axis=0, tiled=True)]
    all_to_all x2 -> x0, waiting for transfers between devices: 64 us -> none  [the longest x1 40.7 us: body(): c = lax.all_to_all(c, ALL, split_axis=0, concat_axis=0, tiled=True)]
    convert_element_type x4 -> x0, local copies, waits for them, and re-layouts: 14.6 us -> none  [the longest x2 9.36 us: body(): (both[0].astype(jnp.float32) + both[1].astype(jnp.float32)).astype(jnp.bf...]
    all_to_all x2 -> x0, starting transfers between devices: 10.3 us -> none  [the longest x1 5.26 us: body(): t = lax.all_to_all(legendre, 'y', split_axis=0, concat_axis=0, tiled=True)]
    dot_general x2 -> x0, matrix products: 9.76 us -> none  [the longest x1 5.18 us: body(): jnp.einsum('iks,ikj->isj', bessel, scaled, preferred_element_type=jnp.flo...]
    transpose x2 -> x0, local copies, waits for them, and re-layouts: 8.9 us -> none  [the longest x1 5.11 us: body(): c = c.reshape(planes, 2, local, per, total).transpose(2, 0, 3, 1, 4)]
    reshape x1 -> x0, local copies, waits for them, and re-layouts: 6.12 us -> none  [body(): coeffs = c.reshape(local, cols, 2, total)]
  transfers between devices with their start and end apart: 2 -> 0, of which waited for: 2 -> 0; matrix products, arithmetic and copies ran while one was open for 3% -> 0% of each run, Pallas kernels for 0% -> 0%
where the time goes in v2:
time: 146 us
  Pallas kernels  138 us (95%)
  local copies, waits for them, and re-layouts  7.61 us (5%)
    pallas_call x1, Pallas kernels, gather(): pl.pallas_call(gather_kernel, out_shape=jax.ShapeDtypeStruct((PER, ND, 24...  108 us
    pallas_call x1, Pallas kernels, radial(): pl.pallas_call(radial_kernel, out_shape=jax.ShapeDtypeStruct((48, 64, 384...  30.7 us
    unnamed x14, local copies, waits for them, and re-layouts  7.39 us

profile of v2, /device:TPU:1, one launch (start us, length us, event | category | flops | bytes accessed | tf_op | source)
XLA Modules:
  0.0 146.0 jit_solution(15645824621082840914)
XLA Ops:
  0.0 0.0 copy-start.1
  0.0 4.1 %copy.11 = bf16[32,2,192,128]{3,0,1,2:T(8,128)(2,1)S(1)} copy(bf16[32,2,192,128]{3,2,1,0:T(8,128)(2,1)} %param.7) | data formatting | bytes 6291456 | tf_op args[0]
  4.1 0.0 copy-done.1
  4.1 0.0 copy-start.4
  4.1 0.0 copy-start.5
  4.1 0.0 copy-start.2
  4.1 0.0 copy-start.3
  4.1 107.5 %gather.1.c_ref = bf16[3,128,24,128]{3,2,1,0:T(8,128)(2,1)S(1)} custom-call(bf16[192,2,32,128]{3,2,1,0:T(8,128)(2,1)S(1)} %bitcast.3, bf16[12,768,128]{2,1,0:T(8,128)(2,1)S(1)} %copy-done.1), custom_call_target="tpu_custom_call" | custom-call | tf_op jit(solution)/shard_map/gather/pallas_call | solution.py:122
  111.7 0.0 copy-done.4
  111.7 0.1 broadcast_in_dim.4
  111.8 0.1 ge.16
  111.9 0.0 copy-done.5
  111.9 0.1 compare_convert_fusion.k_ref
  112.0 0.0 copy-done.2
  112.0 0.0 copy-done.3
  112.0 0.0 copy-start
  112.0 1.9 %copy-done = bf16[6,512,512]{2,1,0:T(8,128)(2,1)S(1)} copy-done((bf16[6,512,512]{2,1,0:T(8,128)(2,1)S(1)}, bf16[6,512,512]{2,1,0:T(8,128)(2,1)}, u32[]{:S(2)}) %copy-start) | copy-done | bytes 3145752
  113.9 30.7 %radial.1 = bf16[48,64,384]{2,1,0:T(8,128)(2,1)S(1)} custom-call(bf16[3,128,24,128]{3,2,1,0:T(8,128)(2,1)S(1)} %gather.1.c_ref, bf16[6,512,512]{2,1,0:T(8,128)(2,1)S(1)} %copy-done, f32[6,512]{1,0:T(8,128)S(1)} %copy-done.2, f32[6,512]{1,0:T(8,128)S(1)} %copy-done.3, f32[6,384]{1,0:T(8,128)S(1)} %compare_convert_fusion.k_ref), custom_call_target="tpu_custom_call" | custom-call | tf_op jit(solution)/shard_map/radial/pallas_call | solution.py:183
  144.6 1.4 copy.13
Async XLA Ops:
  0.0 4.1 %copy-start.1 = (bf16[12,768,128]{2,1,0:T(8,128)(2,1)S(1)}, bf16[12,768,128]{2,1,0:T(8,128)(2,1)}, u32[]{:S(2)}) copy-start(bf16[12,768,128]{2,1,0:T(8,128)(2,1)} %l_ref.1) | copy-start | bytes 7077892
  4.1 107.6 %copy-start.4 = (s32[192]{0:T(256)S(1)}, s32[192]{0:T(256)}, u32[]{:S(2)}) copy-start(s32[192]{0:T(256)} %param.9) | copy-start | bytes 2308
  4.1 107.8 %copy-start.5 = (s32[6]{0:T(128)S(1)}, s32[6]{0:T(128)}, u32[]{:S(2)}) copy-start(s32[6]{0:T(128)} %param.10) | copy-start | bytes 76
  4.1 107.9 %copy-start.2 = (f32[6,512]{1,0:T(8,128)S(1)}, f32[6,512]{1,0:T(8,128)}, u32[]{:S(2)}) copy-start(f32[6,512]{1,0:T(8,128)} %s_ref.1) | copy-start | bytes 36868
  4.1 107.9 %copy-start.3 = (f32[6,512]{1,0:T(8,128)S(1)}, f32[6,512]{1,0:T(8,128)}, u32[]{:S(2)}) copy-start(f32[6,512]{1,0:T(8,128)} %n_ref.1) | copy-start | bytes 36868
  112.0 1.9 %copy-start = (bf16[6,512,512]{2,1,0:T(8,128)(2,1)S(1)}, bf16[6,512,512]{2,1,0:T(8,128)(2,1)}, u32[]{:S(2)}) copy-start(bf16[6,512,512]{2,1,0:T(8,128)(2,1)} %b_ref.1) | copy-start | bytes 9437188

commit v3 on v2

v3 whole, which is shorter than its diff:
```python
import jax
import jax.numpy as jnp
from jax import lax
from jax.experimental import pallas as pl
from jax.experimental.pallas import tpu as pltpu
from jax.sharding import Mesh, PartitionSpec as P

ALL = ("z", "x", "y", "core")
SHELL = ("z", "x")
BLK = ("y", "core")
MESH = pl.DeviceIdType.MESH
BF16, F32 = jnp.bfloat16, jnp.float32
ROWS, CYC, SH = 768, 128, 32
NP, ND, PER = 64, 128, 3


def place():
    return tuple(lax.axis_index(n) for n in ALL)


def remote(src, dst, send, recv, z, x, y, c):
    return pltpu.make_async_remote_copy(
        src_ref=src, dst_ref=dst, send_sem=send, recv_sem=recv,
        device_id=(z, x, y, c), device_id_type=MESH,
    )


def drain(ref, sem):
    pltpu.make_async_copy(ref, ref, sem).wait()


def kernel(f_ref, l_ref, b_ref, s_ref, n_ref, k_ref, out_ref,
           fin, ff, ft, fr, lr, ps, pr, cf, cs, cr, xf, xi, os, bes,
           in_sem, f_send, f_recv, l_send, l_recv, p_send, p_recv, c_send, c_recv, o_send, o_recv):
    z, x, y, c = place()
    plane = (z * 4 + x) * 4 + y
    me = plane * 2 + c
    blk = y * 2 + c
    load = pltpu.make_async_copy(f_ref, fin, in_sem.at[0])
    load.start()
    barrier = pltpu.get_barrier_semaphore()

    def greet(d, _):
        pl.semaphore_signal(
            barrier, inc=1, device_id_type=MESH,
            device_id=((z + d // 32) % 4, (x + d // 8) % 4, (y + d // 2) % 4, (c + d) % 2),
        )
        return 0

    lax.fori_loop(1, ND, greet, 0)
    basis_load = pltpu.make_async_copy(b_ref, bes, in_sem.at[1])
    basis_load.start()
    load.wait()

    def lift(i, _):
        for h in range(2):
            ff[h, pl.ds(i * 192, 192), :] = fin[i, h].astype(F32)
        return 0

    lax.fori_loop(0, SH, lift, 0)
    pl.semaphore_wait(barrier, ND - 1)

    for j in range(PER):
        for d in (2, 1, 3):
            ty = (y + d) % 4
            remote(l_ref.at[ty * PER + j], lr.at[j, y], l_send.at[j], l_recv.at[j], z, x, ty, c).start()
        pltpu.make_async_copy(l_ref.at[y * PER + j], lr.at[j, y], l_recv.at[j]).start()

        def turn(t, _, j=j):
            for h in range(2):
                ft[j, t, h] = ff[h, pl.ds(t * PER + j, SH, stride=192), :].astype(BF16)
            return 0

        lax.fori_loop(0, NP, turn, 0)

        def send(d, _, j=j):
            tz, tx, ty = (z + d // 16) % 4, (x + d // 4) % 4, (y + d) % 4
            t = (tz * 4 + tx) * 4 + ty
            remote(ft.at[j, t], fr.at[j, z * 4 + x, y], f_send.at[j], f_recv.at[j], tz, tx, ty, c).start()
            return 0

        lax.fori_loop(1, NP, send, 0)
        pltpu.make_async_copy(ft.at[j, plane], fr.at[j, z * 4 + x, y], f_recv.at[j]).start()

    def half(j, part, m):
        lhs = jnp.concatenate([lr[j, b, pl.ds(m * 128, 128), :] for b in range(4)], axis=1)
        rhs = jnp.concatenate([fr[j, :, b, part].reshape(16 * SH, CYC) for b in range(4)], axis=1)
        return lax.dot_general(lhs, rhs, (((1,), (1,)), ((), ())), preferred_element_type=F32)

    def spread(j, part):
        def step(m, _):
            acc = half(j, part, m)
            for q in range(4):
                cf[pl.ds(m * 512 + q, 128, stride=4), :] = acc[:, q * 128:(q + 1) * 128]
            return 0

        lax.fori_loop(0, ROWS // 128, step, 0)

    for j in range(PER):
        drain(lr.at[j], l_recv.at[j])
        drain(fr.at[j], f_recv.at[j])
        spread(j, 1 - c)

        def keep(m, _, j=j):
            rows = pl.ds(m * 512, 512)
            ps[j, rows, :] = cf[rows, :].astype(BF16)
            return 0

        lax.fori_loop(0, ROWS // 128, keep, 0)
        swap = remote(ps.at[j], pr.at[j], p_send.at[j], p_recv.at[j], z, x, y, 1 - c)
        swap.start()
        spread(j, c)
        swap.wait_recv()

        def add(m, _, j=j):
            rows = pl.ds(m * 512, 512)
            cs[j, rows, :] = (cf[rows, :] + pr[j, rows, :].astype(F32)).astype(BF16)
            return 0

        lax.fori_loop(0, ROWS // 128, add, 0)

        def post(d, _, j=j):
            tz, tx, ty, tc = (z + d // 32) % 4, (x + d // 8) % 4, (y + d // 2) % 4, (c + d) % 2
            t = ((tz * 4 + tx) * 4 + ty) * 2 + tc
            remote(cs.at[j, pl.ds(t * 24, 24)], cr.at[j, me], c_send.at[j], c_recv.at[j], tz, tx, ty, tc).start()
            return 0

        lax.fori_loop(1, ND, post, 0)
        pltpu.make_async_copy(cs.at[j, pl.ds(me * 24, 24)], cr.at[j, me], c_recv.at[j]).start()

    basis_load.wait()
    for j in range(PER):
        drain(cr.at[j], c_recv.at[j])

        def widen(m, _, j=j):
            xf[pl.ds((j * 8 + m) * 384, 384), :] = cr[j, pl.ds(m * 16, 16)].reshape(384, 128).astype(F32)
            return 0

        lax.fori_loop(0, 8, widen, 0)

    def row(i, _):
        for q in range(4):
            for j in range(PER):
                for h in range(2):
                    xi[q, pl.ds(2 * j + h, 64, stride=6), :] = xf[pl.ds(j * 3072 + h * 24 + i * 4 + q, 64, stride=48), :]
        rows = jnp.concatenate([xi[q].astype(BF16) for q in range(4)], axis=1)
        basis = bes[i]
        forward = lax.dot_general(rows, basis, (((1,), (1,)), ((), ())), preferred_element_type=F32)
        power = s_ref[pl.ds(i, 1), :]
        scaled = (forward * (power / (power + n_ref[pl.ds(i, 1), :]))).astype(BF16)
        out = lax.dot_general(basis, scaled, (((0,), (1,)), ((), ())), preferred_element_type=F32)
        out = jnp.where(k_ref[pl.ds(i, 1), :] > 0.5, out, 0.0)
        os[i] = out.astype(BF16)
        for d in range(1, 8):
            ty, tc = (y + d // 2) % 4, (c + d) % 2
            remote(os.at[i, pl.ds((ty * 2 + tc) * 64, 64)], out_ref.at[blk * 6 + i], o_send, o_recv, z, x, ty, tc).start()
        pltpu.make_async_copy(os.at[i, pl.ds(blk * 64, 64)], out_ref.at[blk * 6 + i], o_recv).start()
        return 0

    lax.fori_loop(0, 6, row, 0)
    for j in range(PER):
        drain(lr.at[j, pl.ds(0, 3)], l_send.at[j])
        drain(ft.at[j, pl.ds(0, NP - 1)], f_send.at[j])
        drain(cr.at[j, pl.ds(0, ND - 1)], c_send.at[j])
        remote(ps.at[j], pr.at[j], p_send.at[j], p_recv.at[j], z, x, y, 1 - c).wait_send()
    drain(out_ref, o_recv)
    drain(out_ref.at[pl.ds(0, 42)], o_send)


def run(f, t, bessel, signal, noise, keep):
    dma = pltpu.SemaphoreType.DMA
    vmem = pltpu.VMEM
    anywhere = pl.BlockSpec(memory_space=pl.ANY)
    inside = pl.BlockSpec(memory_space=vmem)
    return pl.pallas_call(
        kernel,
        out_shape=jax.ShapeDtypeStruct((48, 64, 384), BF16),
        in_specs=[anywhere] * 3 + [inside] * 3,
        out_specs=anywhere,
        scratch_shapes=[
            vmem((SH, 2, 192, CYC), BF16),
            vmem((2, SH * 192, CYC), F32),
            vmem((PER, NP, 2, SH, CYC), BF16),
            vmem((PER, 16, 4, 2, SH, CYC), BF16),
            vmem((PER, 4, ROWS, CYC), BF16),
            vmem((PER, ROWS * 4, 128), BF16),
            vmem((PER, ROWS * 4, 128), BF16),
            vmem((ROWS * 4, 128), F32),
            vmem((PER, ROWS * 4, 128), BF16),
            vmem((PER, ND, 24, 128), BF16),
            vmem((PER * ND * 24, 128), F32),
            vmem((4, 384, 128), F32),
            vmem((6, 512, 384), BF16),
            vmem((6, 512, 512), BF16),
            dma((2,)),
        ] + [dma((PER,))] * 8 + [dma, dma],
        compiler_params=pltpu.CompilerParams(collective_id=0, has_side_effects=True, vmem_limit_bytes=56 * 2**20),
        name="sphere",
    )(f, t, bessel, signal, noise, keep)


def body(cycle_fourier, legendre, azimuth_orders, multipole, bessel, signal_power, noise_power):
    allowed = multipole[:, None] >= jnp.repeat(azimuth_orders, 2)[None, :]
    return run(cycle_fourier, legendre, bessel, signal_power, noise_power, allowed.astype(F32))


def solution(mesh):
    fine = Mesh(mesh.devices.reshape(4, 4, 4, 2), ALL)
    return jax.shard_map(
        body,
        mesh=fine,
        in_specs=(
            P(SHELL, None, None, BLK),
            P(SHELL, None, BLK),
            P(),
            P(ALL),
            P(ALL, None, None),
            P(ALL, None),
            P(ALL, None),
        ),
        out_specs=P(SHELL, BLK, None),
        check_vma=False,
    )
```

time: 146 us -> 143 us (0.979)
  local copies, waits for them, and re-layouts: 7.61 us -> 4.21 us
    unnamed x14 -> x1, local copies, waits for them, and re-layouts: 7.39 us -> 3.31 us
    pallas_call x2 -> x1, Pallas kernels: 138 us -> 137 us  [run(): pl.pallas_call(kernel, out_shape=jax.ShapeDtypeStruct((48, 64, 384), BF16...]
where the time goes in v3:
time: 143 us
  Pallas kernels  137 us (96%)
  local copies, waits for them, and re-layouts  4.21 us (3%)
    pallas_call x1, Pallas kernels, run(): pl.pallas_call(kernel, out_shape=jax.ShapeDtypeStruct((48, 64, 384), BF16...  137 us
    unnamed x1, local copies, waits for them, and re-layouts  3.31 us

profile of v3, /device:TPU:1, one launch (start us, length us, event | category | flops | bytes accessed | tf_op | source)
XLA Modules:
  0.0 142.8 jit_solution(7591108970233953883)
XLA Ops:
  0.0 0.8 broadcast_in_dim.4
  0.8 0.1 ge.16
  0.9 1.3 compare_convert_fusion.k_ref
  2.2 137.2 %sphere.1 = bf16[48,64,384]{2,1,0:T(8,128)(2,1)} custom-call(bf16[32,2,192,128]{3,2,1,0:T(8,128)(2,1)} %f_ref.1, bf16[12,768,128]{2,1,0:T(8,128)(2,1)} %l_ref.1, bf16[6,512,512]{2,1,0:T(8,128)(2,1)} %b_ref.1, f32[6,512]{1,0:T(8,128)} %s_ref.1, f32[6,512]{1,0:T(8,128)} %n_ref.1, f32[6,384]{1,0:T(8,128)} %compare_convert_fusion.k_ref), custom_call_target="tpu_custom_call" | custom-call | tf_op jit(solution)/shard_map/sphere/pallas_call | solution.py:175
  139.4 3.3 %copy.9 = bf16[48,64,384]{2,1,0:T(8,128)(2,1)} copy(bf16[48,64,384]{2,1,0:T(8,128)(2,1)} %sphere.1) | data formatting | bytes 4718592

commit v4 on v3

--- a/solution.py
+++ b/solution.py
@@ -29,9 +29,9 @@
     pltpu.make_async_copy(ref, ref, sem).wait()
 
 
-def kernel(f_ref, l_ref, b_ref, s_ref, n_ref, k_ref, out_ref,
-           fin, ff, ft, fr, lr, ps, pr, cf, cs, cr, xf, xi, os, bes,
-           in_sem, f_send, f_recv, l_send, l_recv, p_send, p_recv, c_send, c_recv, o_send, o_recv):
+def kernel(f_ref, l_ref, b_ref, s_ref, n_ref, a_ref, m_ref, out_ref,
+           fin, ff, ft, fr, lr, ps, pr, cf, cs, cr, xi, os, bes, az,
+           in_sem, f_send, f_recv, l_send, l_recv, p_send, p_recv, c_send, c_recv, o_send, o_recv, plane_in, all_in):
     z, x, y, c = place()
     plane = (z * 4 + x) * 4 + y
     me = plane * 2 + c
@@ -40,38 +40,55 @@
     load.start()
     barrier = pltpu.get_barrier_semaphore()
 
-    def greet(d, _):
+    def tell(sem, dz=0, dx=0, db=0):
         pl.semaphore_signal(
-            barrier, inc=1, device_id_type=MESH,
-            device_id=((z + d // 32) % 4, (x + d // 8) % 4, (y + d // 2) % 4, (c + d) % 2),
+            sem, inc=1, device_id_type=MESH,
+            device_id=((z + dz) % 4, (x + dx) % 4, (y + db // 2) % 4, (c + db) % 2),
         )
-        return 0
-
-    lax.fori_loop(1, ND, greet, 0)
+
+    for d in range(1, 8):
+        tell(barrier, db=d)
+    for d in range(1, 4):
+        tell(barrier, dx=d)
+        tell(barrier, dz=d)
     basis_load = pltpu.make_async_copy(b_ref, bes, in_sem.at[1])
     basis_load.start()
-    load.wait()
-
-    def lift(i, _):
-        for h in range(2):
-            ff[h, pl.ds(i * 192, 192), :] = fin[i, h].astype(F32)
-        return 0
-
-    lax.fori_loop(0, SH, lift, 0)
-    pl.semaphore_wait(barrier, ND - 1)
-
-    for j in range(PER):
+    pl.semaphore_wait(barrier, 13)
+
+    def send_table(j):
         for d in (2, 1, 3):
             ty = (y + d) % 4
             remote(l_ref.at[ty * PER + j], lr.at[j, y], l_send.at[j], l_recv.at[j], z, x, ty, c).start()
         pltpu.make_async_copy(l_ref.at[y * PER + j], lr.at[j, y], l_recv.at[j]).start()
 
+    send_table(0)
+    for d in range(1, 4):
+        tell(plane_in, dx=d)
+    load.wait()
+
+    def lift(i, _):
+        for h in range(2):
+            ff[pl.ds(h * 6144 + i * 192, 192), :] = fin[i, h].astype(F32)
+        return 0
+
+    lax.fori_loop(0, SH // 2, lift, 0)
+    pl.semaphore_wait(plane_in, 3)
+    for d in range(1, 8):
+        tell(all_in, db=d)
+    lax.fori_loop(SH // 2, SH, lift, 0)
+
+    for j in range(PER):
+        if j > 0:
+            send_table(j)
+
         def turn(t, _, j=j):
             for h in range(2):
-                ft[j, t, h] = ff[h, pl.ds(t * PER + j, SH, stride=192), :].astype(BF16)
+                ft[j, t, h] = ff[pl.ds(h * 6144 + t * PER + j, SH, stride=192), :].astype(BF16)
             return 0
 
         lax.fori_loop(0, NP, turn, 0)
+        if j == 0:
+            pl.semaphore_wait(all_in, 7)
 
         def send(d, _, j=j):
             tz, tx, ty = (z + d // 16) % 4, (x + d // 4) % 4, (y + d) % 4
@@ -81,6 +98,15 @@
 
         lax.fori_loop(1, NP, send, 0)
         pltpu.make_async_copy(ft.at[j, plane], fr.at[j, z * 4 + x, y], f_recv.at[j]).start()
+
+    orders = a_ref[...].reshape(1, 192)
+    high = orders // 32
+    pick = (lax.broadcasted_iota(jnp.int32, (192, 384), 1) // 2 == lax.broadcasted_iota(jnp.int32, (192, 384), 0)).astype(BF16)
+    parts = [
+        jnp.dot(jnp.broadcast_to(v.astype(F32), (8, 192)).astype(BF16), pick, preferred_element_type=F32)
+        for v in (high, orders - high * 32)
+    ]
+    az[...] = (parts[0] * 32.0 + parts[1]).astype(jnp.int32)
 
     def half(j, part, m):
         lhs = jnp.concatenate([lr[j, b, pl.ds(m * 128, 128), :] for b in range(4)], axis=1)
@@ -133,7 +159,7 @@
         drain(cr.at[j], c_recv.at[j])
 
         def widen(m, _, j=j):
-            xf[pl.ds((j * 8 + m) * 384, 384), :] = cr[j, pl.ds(m * 16, 16)].reshape(384, 128).astype(F32)
+            ff[pl.ds((j * 8 + m) * 384, 384), :] = cr[j, pl.ds(m * 16, 16)].reshape(384, 128).astype(F32)
             return 0
 
         lax.fori_loop(0, 8, widen, 0)
@@ -142,14 +168,14 @@
         for q in range(4):
             for j in range(PER):
                 for h in range(2):
-                    xi[q, pl.ds(2 * j + h, 64, stride=6), :] = xf[pl.ds(j * 3072 + h * 24 + i * 4 + q, 64, stride=48), :]
+                    xi[q, pl.ds(2 * j + h, 64, stride=6), :] = ff[pl.ds(j * 3072 + h * 24 + i * 4 + q, 64, stride=48), :]
         rows = jnp.concatenate([xi[q].astype(BF16) for q in range(4)], axis=1)
         basis = bes[i]
         forward = lax.dot_general(rows, basis, (((1,), (1,)), ((), ())), preferred_element_type=F32)
         power = s_ref[pl.ds(i, 1), :]
         scaled = (forward * (power / (power + n_ref[pl.ds(i, 1), :]))).astype(BF16)
         out = lax.dot_general(basis, scaled, (((0,), (1,)), ((), ())), preferred_element_type=F32)
-        out = jnp.where(k_ref[pl.ds(i, 1), :] > 0.5, out, 0.0)
+        out = jnp.where(az[0:1, :] <= m_ref[i], out, 0.0)
         os[i] = out.astype(BF16)
         for d in range(1, 8):
             ty, tc = (y + d // 2) % 4, (c + d) % 2
@@ -167,7 +193,7 @@
     drain(out_ref.at[pl.ds(0, 42)], o_send)
 
 
-def run(f, t, bessel, signal, noise, keep):
+def run(f, t, bessel, signal, noise, orders, multipole):
     dma = pltpu.SemaphoreType.DMA
     vmem = pltpu.VMEM
     anywhere = pl.BlockSpec(memory_space=pl.ANY)
@@ -175,11 +201,11 @@
     return pl.pallas_call(
         kernel,
         out_shape=jax.ShapeDtypeStruct((48, 64, 384), BF16),
-        in_specs=[anywhere] * 3 + [inside] * 3,
+        in_specs=[pl.BlockSpec(memory_space=pltpu.HBM)] * 3 + [inside] * 3 + [pl.BlockSpec(memory_space=pltpu.SMEM)],
         out_specs=anywhere,
         scratch_shapes=[
             vmem((SH, 2, 192, CYC), BF16),
-            vmem((2, SH * 192, CYC), F32),
+            vmem((2 * SH * 192, CYC), F32),
             vmem((PER, NP, 2, SH, CYC), BF16),
             vmem((PER, 16, 4, 2, SH, CYC), BF16),
             vmem((PER, 4, ROWS, CYC), BF16),
@@ -188,20 +214,19 @@
             vmem((ROWS * 4, 128), F32),
             vmem((PER, ROWS * 4, 128), BF16),
             vmem((PER, ND, 24, 128), BF16),
-            vmem((PER * ND * 24, 128), F32),
             vmem((4, 384, 128), F32),
             vmem((6, 512, 384), BF16),
             vmem((6, 512, 512), BF16),
+            vmem((8, 384), jnp.int32),
             dma((2,)),
-        ] + [dma((PER,))] * 8 + [dma, dma],
-        compiler_params=pltpu.CompilerParams(collective_id=0, has_side_effects=True, vmem_limit_bytes=56 * 2**20),
+        ] + [dma((PER,))] * 8 + [dma, dma, pltpu.SemaphoreType.REGULAR, pltpu.SemaphoreType.REGULAR],
+        compiler_params=pltpu.CompilerParams(collective_id=0, has_side_effects=True, vmem_limit_bytes=50 * 2**20),
         name="sphere",
-    )(f, t, bessel, signal, noise, keep)
+    )(f, t, bessel, signal, noise, orders, multipole)
 
 
 def body(cycle_fourier, legendre, azimuth_orders, multipole, bessel, signal_power, noise_power):
-    allowed = multipole[:, None] >= jnp.repeat(azimuth_orders, 2)[None, :]
-    return run(cycle_fourier, legendre, bessel, signal_power, noise_power, allowed.astype(F32))
+    return run(cycle_fourier, legendre, bessel, signal_power, noise_power, azimuth_orders, multipole)
 
 
 def solution(mesh):

time: 143 us -> 138 us (0.965)
  Pallas kernels: 137 us -> 133 us
    pallas_call x1, Pallas kernels: 137 us -> 133 us  [run(): pl.pallas_call(kernel, out_shape=jax.ShapeDtypeStruct((48, 64, 384), BF16...]
    unnamed x1 -> x9, local copies, waits for them, and re-layouts: 3.31 us -> 4.17 us
where the time goes in v4:
time: 138 us; the launch traced here: 137 us
  Pallas kernels  133 us (96%)
  local copies, waits for them, and re-layouts  4.17 us (3%)
    pallas_call x1, Pallas kernels, run(): pl.pallas_call(kernel, out_shape=jax.ShapeDtypeStruct((48, 64, 384), BF16...  133 us
    unnamed x9, local copies, waits for them, and re-layouts  4.17 us

profile of v4, /device:TPU:1, one launch (start us, length us, event | category | flops | bytes accessed | tf_op | source)
XLA Modules:
  0.0 137.3 jit_solution(11926037334119825227)
XLA Ops:
  0.0 0.0 copy-start
  0.0 0.7 copy-done
  0.7 0.0 copy-start.1
  0.7 0.7 copy-done.1
  1.4 0.0 copy-start.2
  1.4 0.7 copy-done.2
  2.1 0.0 copy-start.3
  2.1 0.7 copy-done.3
  2.8 133.1 %sphere.1 = bf16[48,64,384]{2,1,0:T(8,128)(2,1)S(1)} custom-call(bf16[32,2,192,128]{3,2,1,0:T(8,128)(2,1)} %f_ref.1, bf16[12,768,128]{2,1,0:T(8,128)(2,1)} %l_ref.1, bf16[6,512,512]{2,1,0:T(8,128)(2,1)} %b_ref.1, f32[6,512]{1,0:T(8,128)S(1)} %copy-done, f32[6,512]{1,0:T(8,128)S(1)} %copy-done.1, s32[192]{0:T(256)S(1)} %copy-done.2, s32[6]{0:T(128)S(1)} %copy-done.3), custom_call_target="tpu_custom_call" | custom-call | tf_op jit(solution)/shard_map/sphere/pallas_call | solution.py:201
  135.9 1.4 %copy.9 = bf16[48,64,384]{2,1,0:T(8,128)(2,1)} copy(bf16[48,64,384]{2,1,0:T(8,128)(2,1)S(1)} %sphere.1) | data formatting | bytes 4718592
Async XLA Ops:
  0.0 0.7 copy-start
  0.7 0.7 copy-start.1
  1.4 0.7 copy-start.2
  2.1 0.7 copy-start.3
